TPU v7x, 512 devices: a whole 4x8x8 slice. The times are simulated.
512 devices in a mesh: node: 64 (over y_hi, z, x), head: 8 (over y_lo, core).
Axes of the slice: x: 4, y: 8 (y_hi: 2, y_lo: 4; y = y_hi * 4 + y_lo), z: 8, core: 2. Of those that a mesh axis runs over, the one named last changes fastest.
Arguments:
- features: bfloat16 [8192, 128], P('node'), may hold values from -1201 to 1201
- proj_weight: bfloat16 [128, 1024], P(None, 'head'), may hold values from -1 to 1
- score_source: float32 [8, 128], P('head'), may hold values from -1 to 1
- score_target: float32 [8, 128], P('head'), may hold values from -1 to 1
- out_weight: bfloat16 [1024, 256], P('head'), may hold values from -0.1875 to 0.1875
- presence: int32 [64, 64], P('node'), may hold values from 0 to 1, as said below
- tile_masks: int32 [64, 16, 128, 128], P('node'), may hold values 0 or 1
Outputs:
- mixed: bfloat16 [8192, 256], P('node')
Inputs may be any that keep to these rules, and one draw needn't show every extreme that they name: Each row holds exactly 16 ones; tile_masks[r, k] belongs to the k-th present tile of row r of presence, counted in ascending order of tile.
All inputs are finite; a program needn't handle non-finite values. No bound on the sum of `tile_masks` on one device may be relied on, other than what follows from the above.
Results may differ from a plain program's by a relative error of at most 0.015.
Values may be sent and summed in bfloat16 or wider, within the bound.
No kernel may reach another device: no remote copies, remote signals or barrier semaphores. Data moves between devices by JAX's collectives and lax.ppermute only.
A program may use at most 64 MiB of HBM per device.

v0:
```python
import math
import jax
import jax.numpy as jnp
from jax import lax
from jax.sharding import PartitionSpec as P


def leaky_relu(values):
    return jnp.where(values > 0, values, 0.2 * values)


def per_device(features, proj_weight, score_source, score_target, out_weight, presence, tile_masks):
    target_count = features.shape[0]
    heads_here = score_source.shape[0]
    head_width = score_source.shape[1]
    tile_width = tile_masks.shape[-1]
    row_tiles = presence.shape[0]

    def project(rows):
        return jnp.dot(rows, proj_weight, preferred_element_type=jnp.float32).astype(jnp.bfloat16)

    def head_terms(projected, vectors):
        widened = lax.optimization_barrier(projected).astype(jnp.float32)
        widened = widened.reshape(projected.shape[0], heads_here, head_width)
        return jnp.sum(widened * vectors[None], axis=-1).T

    local_proj = project(features)
    target_terms = head_terms(local_proj, score_target)
    first_row = lax.axis_index("node") * target_count
    target_ids = first_row + jnp.arange(target_count, dtype=jnp.int32)
    slots = jnp.maximum(jnp.cumsum(presence, axis=1) - 1, 0)
    tile_rows = jnp.arange(row_tiles, dtype=jnp.int32)

    def absorb(carry, block):
        running, denominator, accum = carry
        block_values, block_source, block_start = block
        span_rows = block_values.shape[0]
        column_ids = block_start + jnp.arange(span_rows, dtype=jnp.int32)
        column_tiles = column_ids // tile_width
        column_lanes = column_ids % tile_width
        present_here = jnp.take(presence, column_tiles, axis=1)
        slot_here = jnp.take(slots, column_tiles, axis=1)
        gathered = tile_masks[tile_rows[:, None], slot_here, :, column_lanes[None, :]]
        tile_bits = (
            (gathered * present_here[:, :, None])
            .transpose(0, 2, 1)
            .reshape(target_count, span_rows)
        )
        itself = column_ids[None, :] == target_ids[:, None]
        linked = (tile_bits == 1) & jnp.logical_not(itself) | itself
        edge_scores = leaky_relu(target_terms[:, :, None] + block_source[:, None, :])
        edge_scores = jnp.where(linked[None], edge_scores, -1e30)
        new_peak = jnp.maximum(running, jnp.max(edge_scores, axis=-1))
        edge_weights = jnp.where(linked[None], jnp.exp(edge_scores - new_peak[:, :, None]), 0.0)
        factor = jnp.exp(running - new_peak)
        denominator = denominator * factor + jnp.sum(edge_weights, axis=-1)
        update = jnp.einsum(
            "htb,bhd->htd",
            edge_weights.astype(jnp.bfloat16),
            block_values.reshape(span_rows, heads_here, head_width),
            preferred_element_type=jnp.float32,
        )
        accum = accum * factor[:, :, None] + update
        return ((new_peak, denominator, accum), None)

    initial = (
        jnp.full((heads_here, target_count), -1e30, jnp.float32),
        jnp.zeros((heads_here, target_count), jnp.float32),
        jnp.zeros((heads_here, target_count, head_width), jnp.float32),
    )
    carry = initial
    block_values = project(lax.all_gather(features, "node", axis=0, tiled=True))
    total_rows = block_values.shape[0]
    stride = math.gcd(total_rows, 1024)
    blocks = total_rows // stride
    block_source = head_terms(block_values, score_source)
    stacked = (
        block_values.reshape(blocks, stride, heads_here * head_width),
        block_source.reshape(heads_here, blocks, stride).transpose(1, 0, 2),
        stride * jnp.arange(blocks, dtype=jnp.int32),
    )
    carry, unused = lax.scan(absorb, carry, stacked)
    running, denominator, accum = carry
    heads_out = jax.nn.elu(accum / denominator[:, :, None]).astype(jnp.bfloat16)
    heads_out = heads_out.transpose(1, 0, 2).reshape(target_count, heads_here * head_width)
    partial_sum = jnp.dot(heads_out, out_weight, preferred_element_type=jnp.float32)
    result = lax.psum(partial_sum.astype(jnp.bfloat16), "head")
    return result


def solution(mesh):
    return jax.shard_map(
        per_device,
        mesh=mesh,
        in_specs=(
            P("node", None),
            P(None, "head"),
            P("head", None),
            P("head", None),
            P("head", None),
            P("node", None),
            P("node", None, None, None),
        ),
        out_specs=P("node", None),
        check_vma=False,
    )
```

profile of v0, /device:TPU:2, one launch (start us, length us, event | category | flops | bytes accessed | tf_op | source)
XLA Modules:
  0.0 1015.9 jit_solution(6120727612200111464)
XLA Ops:
  7.4 1.6 copy.9
  9.5 140.4 %all-gather.2.cloned.1.call-done = bf16[8192,128]{1,0:T(8,128)(2,1)} async-done(((bf16[128,128]{1,0:T(8,128)(2,1)}), bf16[8192,128]{1,0:T(8,128)(2,1)}) %all-gather.2.cloned.1.call-update) | async-done | bytes 2097168 | tf_op jit(solution)/shard_map/all_gather | solution.py:72
  149.8 2.3 convolution_convert_fusion
  153.5 781.3 %while.17 = (s32[]{:T(128)}, f32[1,128]{1,0:T(1,128)S(1)}, f32[1,128]{1,0:T(1,128)S(1)}, f32[1,128,128]{2,1,0:T(8,128)S(1)}, s32[8]{0:T(128)S(1)}, /*index=5*/s3...) while((s32[]{:T(128)}, f32[1,128]{1,0:T(1,128)S(1)}, ...), condition=%wide.region_6.8_spmd.clone, body=%wide.region_3.7_spmd.clone.sunk | while | flops 37613440 | bytes 2482873 | solution.py:82
  157.0 40.4 %select_select_fusion.5 = s32[1024]{0:T(1024)S(1)} fusion(s32[]{:T(128)} %bitcast.403, s32[]{:T(128)} %bitcast.404, s32[]{:T(128)} %bitcast.405, s32[]{:T(128)} %bitcast.406, s32[]{:T(128)} %bitcast.407, s32[]{:T(128)} %bitcast.408, s32[]{:T(128)} %bitcast.409, s32[]{:T(128)} %bitcast.410, s32[]{:T(128)} %bitcast.411, s32[]{:T(128)} %bitcast.412, ...), kind=kLoop, calls=%fused_computation.49.clone.1 | loop fusion | flops 152576 | bytes 4356 | tf_op jit(solution)/shard_map/while/body/eval_jaxpr/jit(_take)/select_n | solution.py:42
  198.2 6.8 gather_fusion
  207.2 40.6 %select_select_fusion.4 = s32[1024]{0:T(1024)S(1)} fusion(s32[]{:T(128)} %bitcast.339, s32[]{:T(128)} %bitcast.340, s32[]{:T(128)} %bitcast.341, s32[]{:T(128)} %bitcast.342, s32[]{:T(128)} %bitcast.343, s32[]{:T(128)} %bitcast.344, s32[]{:T(128)} %bitcast.345, s32[]{:T(128)} %bitcast.346, s32[]{:T(128)} %bitcast.347, s32[]{:T(128)} %bitcast.348, ...), kind=kLoop, calls=%fused_computation.48.clone.1 | loop fusion | flops 152576 | bytes 4356 | tf_op jit(solution)/shard_map/while/body/eval_jaxpr/jit(_take)/select_n | solution.py:41
  254.7 40.4 %select_select_fusion.5 = s32[1024]{0:T(1024)S(1)} fusion(s32[]{:T(128)} %bitcast.403, s32[]{:T(128)} %bitcast.404, s32[]{:T(128)} %bitcast.405, s32[]{:T(128)} %bitcast.406, s32[]{:T(128)} %bitcast.407, s32[]{:T(128)} %bitcast.408, s32[]{:T(128)} %bitcast.409, s32[]{:T(128)} %bitcast.410, s32[]{:T(128)} %bitcast.411, s32[]{:T(128)} %bitcast.412, ...), kind=kLoop, calls=%fused_computation.49.clone.1 | loop fusion | flops 152576 | bytes 4356 | tf_op jit(solution)/shard_map/while/body/eval_jaxpr/jit(_take)/select_n | solution.py:42
  295.9 6.8 gather_fusion
  304.9 40.6 %select_select_fusion.4 = s32[1024]{0:T(1024)S(1)} fusion(s32[]{:T(128)} %bitcast.339, s32[]{:T(128)} %bitcast.340, s32[]{:T(128)} %bitcast.341, s32[]{:T(128)} %bitcast.342, s32[]{:T(128)} %bitcast.343, s32[]{:T(128)} %bitcast.344, s32[]{:T(128)} %bitcast.345, s32[]{:T(128)} %bitcast.346, s32[]{:T(128)} %bitcast.347, s32[]{:T(128)} %bitcast.348, ...), kind=kLoop, calls=%fused_computation.48.clone.1 | loop fusion | flops 152576 | bytes 4356 | tf_op jit(solution)/shard_map/while/body/eval_jaxpr/jit(_take)/select_n | solution.py:41
  347.0 1.5 fusion.87
  352.3 40.4 %select_select_fusion.5 = s32[1024]{0:T(1024)S(1)} fusion(s32[]{:T(128)} %bitcast.403, s32[]{:T(128)} %bitcast.404, s32[]{:T(128)} %bitcast.405, s32[]{:T(128)} %bitcast.406, s32[]{:T(128)} %bitcast.407, s32[]{:T(128)} %bitcast.408, s32[]{:T(128)} %bitcast.409, s32[]{:T(128)} %bitcast.410, s32[]{:T(128)} %bitcast.411, s32[]{:T(128)} %bitcast.412, ...), kind=kLoop, calls=%fused_computation.49.clone.1 | loop fusion | flops 152576 | bytes 4356 | tf_op jit(solution)/shard_map/while/body/eval_jaxpr/jit(_take)/select_n | solution.py:42
  393.6 6.8 gather_fusion
  402.6 40.6 %select_select_fusion.4 = s32[1024]{0:T(1024)S(1)} fusion(s32[]{:T(128)} %bitcast.339, s32[]{:T(128)} %bitcast.340, s32[]{:T(128)} %bitcast.341, s32[]{:T(128)} %bitcast.342, s32[]{:T(128)} %bitcast.343, s32[]{:T(128)} %bitcast.344, s32[]{:T(128)} %bitcast.345, s32[]{:T(128)} %bitcast.346, s32[]{:T(128)} %bitcast.347, s32[]{:T(128)} %bitcast.348, ...), kind=kLoop, calls=%fused_computation.48.clone.1 | loop fusion | flops 152576 | bytes 4356 | tf_op jit(solution)/shard_map/while/body/eval_jaxpr/jit(_take)/select_n | solution.py:41
  450.0 40.4 %select_select_fusion.5 = s32[1024]{0:T(1024)S(1)} fusion(s32[]{:T(128)} %bitcast.403, s32[]{:T(128)} %bitcast.404, s32[]{:T(128)} %bitcast.405, s32[]{:T(128)} %bitcast.406, s32[]{:T(128)} %bitcast.407, s32[]{:T(128)} %bitcast.408, s32[]{:T(128)} %bitcast.409, s32[]{:T(128)} %bitcast.410, s32[]{:T(128)} %bitcast.411, s32[]{:T(128)} %bitcast.412, ...), kind=kLoop, calls=%fused_computation.49.clone.1 | loop fusion | flops 152576 | bytes 4356 | tf_op jit(solution)/shard_map/while/body/eval_jaxpr/jit(_take)/select_n | solution.py:42
  491.2 6.8 gather_fusion
  500.2 40.6 %select_select_fusion.4 = s32[1024]{0:T(1024)S(1)} fusion(s32[]{:T(128)} %bitcast.339, s32[]{:T(128)} %bitcast.340, s32[]{:T(128)} %bitcast.341, s32[]{:T(128)} %bitcast.342, s32[]{:T(128)} %bitcast.343, s32[]{:T(128)} %bitcast.344, s32[]{:T(128)} %bitcast.345, s32[]{:T(128)} %bitcast.346, s32[]{:T(128)} %bitcast.347, s32[]{:T(128)} %bitcast.348, ...), kind=kLoop, calls=%fused_computation.48.clone.1 | loop fusion | flops 152576 | bytes 4356 | tf_op jit(solution)/shard_map/while/body/eval_jaxpr/jit(_take)/select_n | solution.py:41
  547.7 40.4 %select_select_fusion.5 = s32[1024]{0:T(1024)S(1)} fusion(s32[]{:T(128)} %bitcast.403, s32[]{:T(128)} %bitcast.404, s32[]{:T(128)} %bitcast.405, s32[]{:T(128)} %bitcast.406, s32[]{:T(128)} %bitcast.407, s32[]{:T(128)} %bitcast.408, s32[]{:T(128)} %bitcast.409, s32[]{:T(128)} %bitcast.410, s32[]{:T(128)} %bitcast.411, s32[]{:T(128)} %bitcast.412, ...), kind=kLoop, calls=%fused_computation.49.clone.1 | loop fusion | flops 152576 | bytes 4356 | tf_op jit(solution)/shard_map/while/body/eval_jaxpr/jit(_take)/select_n | solution.py:42
  588.9 6.8 gather_fusion
  597.9 40.6 %select_select_fusion.4 = s32[1024]{0:T(1024)S(1)} fusion(s32[]{:T(128)} %bitcast.339, s32[]{:T(128)} %bitcast.340, s32[]{:T(128)} %bitcast.341, s32[]{:T(128)} %bitcast.342, s32[]{:T(128)} %bitcast.343, s32[]{:T(128)} %bitcast.344, s32[]{:T(128)} %bitcast.345, s32[]{:T(128)} %bitcast.346, s32[]{:T(128)} %bitcast.347, s32[]{:T(128)} %bitcast.348, ...), kind=kLoop, calls=%fused_computation.48.clone.1 | loop fusion | flops 152576 | bytes 4356 | tf_op jit(solution)/shard_map/while/body/eval_jaxpr/jit(_take)/select_n | solution.py:41
  645.3 40.4 %select_select_fusion.5 = s32[1024]{0:T(1024)S(1)} fusion(s32[]{:T(128)} %bitcast.403, s32[]{:T(128)} %bitcast.404, s32[]{:T(128)} %bitcast.405, s32[]{:T(128)} %bitcast.406, s32[]{:T(128)} %bitcast.407, s32[]{:T(128)} %bitcast.408, s32[]{:T(128)} %bitcast.409, s32[]{:T(128)} %bitcast.410, s32[]{:T(128)} %bitcast.411, s32[]{:T(128)} %bitcast.412, ...), kind=kLoop, calls=%fused_computation.49.clone.1 | loop fusion | flops 152576 | bytes 4356 | tf_op jit(solution)/shard_map/while/body/eval_jaxpr/jit(_take)/select_n | solution.py:42
  686.6 6.8 gather_fusion
  695.6 40.6 %select_select_fusion.4 = s32[1024]{0:T(1024)S(1)} fusion(s32[]{:T(128)} %bitcast.339, s32[]{:T(128)} %bitcast.340, s32[]{:T(128)} %bitcast.341, s32[]{:T(128)} %bitcast.342, s32[]{:T(128)} %bitcast.343, s32[]{:T(128)} %bitcast.344, s32[]{:T(128)} %bitcast.345, s32[]{:T(128)} %bitcast.346, s32[]{:T(128)} %bitcast.347, s32[]{:T(128)} %bitcast.348, ...), kind=kLoop, calls=%fused_computation.48.clone.1 | loop fusion | flops 152576 | bytes 4356 | tf_op jit(solution)/shard_map/while/body/eval_jaxpr/jit(_take)/select_n | solution.py:41
  743.0 40.4 %select_select_fusion.5 = s32[1024]{0:T(1024)S(1)} fusion(s32[]{:T(128)} %bitcast.403, s32[]{:T(128)} %bitcast.404, s32[]{:T(128)} %bitcast.405, s32[]{:T(128)} %bitcast.406, s32[]{:T(128)} %bitcast.407, s32[]{:T(128)} %bitcast.408, s32[]{:T(128)} %bitcast.409, s32[]{:T(128)} %bitcast.410, s32[]{:T(128)} %bitcast.411, s32[]{:T(128)} %bitcast.412, ...), kind=kLoop, calls=%fused_computation.49.clone.1 | loop fusion | flops 152576 | bytes 4356 | tf_op jit(solution)/shard_map/while/body/eval_jaxpr/jit(_take)/select_n | solution.py:42
  784.2 6.8 gather_fusion
  793.2 40.6 %select_select_fusion.4 = s32[1024]{0:T(1024)S(1)} fusion(s32[]{:T(128)} %bitcast.339, s32[]{:T(128)} %bitcast.340, s32[]{:T(128)} %bitcast.341, s32[]{:T(128)} %bitcast.342, s32[]{:T(128)} %bitcast.343, s32[]{:T(128)} %bitcast.344, s32[]{:T(128)} %bitcast.345, s32[]{:T(128)} %bitcast.346, s32[]{:T(128)} %bitcast.347, s32[]{:T(128)} %bitcast.348, ...), kind=kLoop, calls=%fused_computation.48.clone.1 | loop fusion | flops 152576 | bytes 4356 | tf_op jit(solution)/shard_map/while/body/eval_jaxpr/jit(_take)/select_n | solution.py:41
  835.3 1.5 fusion.87
  840.7 40.4 %select_select_fusion.5 = s32[1024]{0:T(1024)S(1)} fusion(s32[]{:T(128)} %bitcast.403, s32[]{:T(128)} %bitcast.404, s32[]{:T(128)} %bitcast.405, s32[]{:T(128)} %bitcast.406, s32[]{:T(128)} %bitcast.407, s32[]{:T(128)} %bitcast.408, s32[]{:T(128)} %bitcast.409, s32[]{:T(128)} %bitcast.410, s32[]{:T(128)} %bitcast.411, s32[]{:T(128)} %bitcast.412, ...), kind=kLoop, calls=%fused_computation.49.clone.1 | loop fusion | flops 152576 | bytes 4356 | tf_op jit(solution)/shard_map/while/body/eval_jaxpr/jit(_take)/select_n | solution.py:42
  881.9 6.8 gather_fusion
  890.9 40.6 %select_select_fusion.4 = s32[1024]{0:T(1024)S(1)} fusion(s32[]{:T(128)} %bitcast.339, s32[]{:T(128)} %bitcast.340, s32[]{:T(128)} %bitcast.341, s32[]{:T(128)} %bitcast.342, s32[]{:T(128)} %bitcast.343, s32[]{:T(128)} %bitcast.344, s32[]{:T(128)} %bitcast.345, s32[]{:T(128)} %bitcast.346, s32[]{:T(128)} %bitcast.347, s32[]{:T(128)} %bitcast.348, ...), kind=kLoop, calls=%fused_computation.48.clone.1 | loop fusion | flops 152576 | bytes 4356 | tf_op jit(solution)/shard_map/while/body/eval_jaxpr/jit(_take)/select_n | solution.py:41
  935.7 71.9 %all-reduce.2.cloned.1.call-done = bf16[128,256]{1,0:T(8,128)(2,1)} async-done(((bf16[128,256]{1,0:T(8,128)(2,1)}), bf16[128,256]{1,0:T(8,128)(2,1)}) %all-reduce.2.cloned.1.call-update) | async-done | bytes 65552 | tf_op jit(solution)/shard_map/psum | solution.py:87
  1007.6 1.5 copy.26
  (202 shorter events, 78.1 us)
Async XLA Ops:
  6.5 928.3 %copy-start = (bf16[128,256]{1,0:T(8,128)(2,1)S(1)}, bf16[128,256]{1,0:T(8,128)(2,1)}, u32[]{:S(2)}) copy-start(bf16[128,256]{1,0:T(8,128)(2,1)} %param.15) | copy-start | bytes 196612
  6.5 2.4 copy-start.4
  6.5 2.4 copy-start.3
  6.5 2.5 copy-start.1
  6.5 2.8 copy-start.5
  6.5 143.3 %all-gather.2.cloned.1.call-start = ((), (), s32[]{:S(2)}) async-start(), calls=%async_computation | async-start | bytes 2129920 | tf_op jit(solution)/shard_map/all_gather | solution.py:72
  7.3 1000.3 %all-reduce.2.cloned.1.call-start = ((), (), s32[]{:S(2)}) async-start(), calls=%async_computation.1 | async-start | bytes 131072 | tf_op jit(solution)/shard_map/psum | solution.py:87
  9.5 142.7 %copy-start.6 = (f32[1,128]{1,0:T(1,128)S(1)}, f32[1,128]{1,0:T(1,128)}, u32[]{:S(2)}) copy-start(f32[1,128]{1,0:T(1,128)} %param.13) | copy-start | bytes 1540
  152.1 1.3 copy-start.2
Sparse Core Ops, SparseCore 0:
  11.7 138.0 all-gather.1
  935.8 71.6 all-reduce.1
where the time goes:
time: 1030 us; the launch traced here: 1020 us
  other arithmetic  670 us (65%)
  waiting for transfers between devices  213 us (21%)
  local copies, waits for them, and re-layouts  104 us (10%)
  matrix products  14.9 us (1%)
  between operations  13.5 us (1%)
    select_n x8, other arithmetic, absorb(): present_here = jnp.take(presence, column_tiles, axis=1)  325 us
    select_n x8, other arithmetic, absorb(): slot_here = jnp.take(slots, column_tiles, axis=1)  323 us
    all_gather x1, waiting for transfers between devices, per_device(): block_values = project(lax.all_gather(features, 'node', axis=0, tiled=True))  140 us
    psum x1, waiting for transfers between devices, per_device(): result = lax.psum(partial_sum.astype(jnp.bfloat16), 'head')  71.9 us
    gather x8, local copies, waits for them, and re-layouts, absorb(): tile_masks[tile_rows[:, None], slot_here, :, column_lanes[None, :]]  54.3 us
    gather x32, local copies, waits for them, and re-layouts, absorb(): slot_here = jnp.take(slots, column_tiles, axis=1)  23.1 us
  transfers between devices with their start and end apart: 2, of which 2 were waited for; matrix products, arithmetic and copies ran while one was open for 0% of the time, Pallas kernels for 0%

commit v1 on v0

--- a/solution.py
+++ b/solution.py
@@ -69,7 +69,11 @@
         jnp.zeros((heads_here, target_count, head_width), jnp.float32),
     )
     carry = initial
-    block_values = project(lax.all_gather(features, "node", axis=0, tiled=True))
+    block_values = project(
+        jnp.concatenate(
+            lax.all_to_all(jnp.stack([features] * lax.axis_size("node")), "node", 0, 0), axis=0
+        )
+    )
     total_rows = block_values.shape[0]
     stride = math.gcd(total_rows, 1024)
     blocks = total_rows // stride

time: 1030 us -> 957 us (0.929)
  waiting for transfers between devices: 213 us -> 127 us
  starting transfers between devices: 0.08 us -> 19.2 us
    all_gather x1 -> x0, waiting for transfers between devices: 140 us -> none  [per_device(): block_values = project(lax.all_gather(features, 'node', axis=0, tiled=True))]
    all_to_all x0 -> x1, waiting for transfers between devices: none -> 46.2 us  [per_device(): lax.all_to_all(jnp.stack([features] * lax.axis_size('node')), 'node', 0, 0)]
    all_to_all x0 -> x1, starting transfers between devices: none -> 19.1 us  [per_device(): lax.all_to_all(jnp.stack([features] * lax.axis_size('node')), 'node', 0, 0)]
where the time goes in v1:
time: 957 us; the launch traced here: 947 us
  other arithmetic  667 us (70%)
  waiting for transfers between devices  127 us (13%)
  local copies, waits for them, and re-layouts  105 us (11%)
  starting transfers between devices  19.2 us (2%)
  between operations  13.6 us (1%)
  matrix products  13.3 us (1%)
    select_n x8, other arithmetic, absorb(): present_here = jnp.take(presence, column_tiles, axis=1)  325 us
    select_n x8, other arithmetic, absorb(): slot_here = jnp.take(slots, column_tiles, axis=1)  323 us
    psum x1, waiting for transfers between devices, per_device(): result = lax.psum(partial_sum.astype(jnp.bfloat16), 'head')  81 us
    gather x8, local copies, waits for them, and re-layouts, absorb(): tile_masks[tile_rows[:, None], slot_here, :, column_lanes[None, :]]  54.3 us
    all_to_all x1, waiting for transfers between devices, per_device(): lax.all_to_all(jnp.stack([features] * lax.axis_size('node')), 'node', 0, 0)  46.2 us
    gather x32, local copies, waits for them, and re-layouts, absorb(): slot_here = jnp.take(slots, column_tiles, axis=1)  23.1 us
  transfers between devices with their start and end apart: 2, of which 2 were waited for; matrix products, arithmetic and copies ran while one was open for 0% of the time, Pallas kernels for 0%

profile of v1, /device:TPU:2, one launch (start us, length us, event | category | flops | bytes accessed | tf_op | source)
XLA Modules:
  0.0 947.0 jit_solution(8354182267524966070)
XLA Ops:
  6.5 2.6 stack.2
  9.2 19.1 %all-to-all-start = ((bf16[64,128,128]{2,1,0:T(8,128)(2,1)}), bf16[64,128,128]{2,1,0:T(8,128)(2,1)S(1)}, u32[]{:S(2)}, u32[]{:S(2)}) async-start(bf16[64,128,128]{2,1,0:T(8,128)(2,1)} %stack.2), calls=%async_computation | async-start | bytes 4194304 | tf_op jit(solution)/shard_map/all_to_all | solution.py:74
  28.4 1.6 copy.9
  30.5 46.2 %all-to-all-done = bf16[64,128,128]{2,1,0:T(8,128)(2,1)S(1)} async-done(((bf16[64,128,128]{2,1,0:T(8,128)(2,1)}), bf16[64,128,128]{2,1,0:T(8,128)(2,1)S(1)}, u32[]{:S(2)}, u32[]{:S(2)}) %all-to-all-start) | async-done | bytes 2097184 | tf_op jit(solution)/shard_map/all_to_all | solution.py:74
  78.7 778.0 %while.17 = (s32[]{:T(128)}, f32[1,128]{1,0:T(1,128)S(1)}, f32[1,128]{1,0:T(1,128)S(1)}, f32[1,128,128]{2,1,0:T(8,128)S(1)}, s32[8]{0:T(128)S(1)}, /*index=5*/s3...) while((s32[]{:T(128)}, f32[1,128]{1,0:T(1,128)S(1)}, ...), condition=%wide.region_6.8_spmd.clone, body=%wide.region_3.7_spmd.clone.sunk | while | flops 37613440 | bytes 2482873 | solution.py:86
  82.2 40.3 %select_select_fusion.5 = s32[1024]{0:T(1024)S(1)} fusion(s32[]{:T(128)} %bitcast.404, s32[]{:T(128)} %bitcast.405, s32[]{:T(128)} %bitcast.406, s32[]{:T(128)} %bitcast.407, s32[]{:T(128)} %bitcast.408, s32[]{:T(128)} %bitcast.409, s32[]{:T(128)} %bitcast.410, s32[]{:T(128)} %bitcast.411, s32[]{:T(128)} %bitcast.412, s32[]{:T(128)} %bitcast.413, ...), kind=kLoop, calls=%fused_computation.49.clone.1 | loop fusion | flops 152576 | bytes 4356 | tf_op jit(solution)/shard_map/while/body/eval_jaxpr/jit(_take)/select_n | solution.py:42
  123.2 6.8 gather_fusion
  132.2 40.6 %select_select_fusion.4 = s32[1024]{0:T(1024)S(1)} fusion(s32[]{:T(128)} %bitcast.340, s32[]{:T(128)} %bitcast.341, s32[]{:T(128)} %bitcast.342, s32[]{:T(128)} %bitcast.343, s32[]{:T(128)} %bitcast.344, s32[]{:T(128)} %bitcast.345, s32[]{:T(128)} %bitcast.346, s32[]{:T(128)} %bitcast.347, s32[]{:T(128)} %bitcast.348, s32[]{:T(128)} %bitcast.349, ...), kind=kLoop, calls=%fused_computation.48.clone.1 | loop fusion | flops 152576 | bytes 4356 | tf_op jit(solution)/shard_map/while/body/eval_jaxpr/jit(_take)/select_n | solution.py:41
  179.5 40.3 %select_select_fusion.5 = s32[1024]{0:T(1024)S(1)} fusion(s32[]{:T(128)} %bitcast.404, s32[]{:T(128)} %bitcast.405, s32[]{:T(128)} %bitcast.406, s32[]{:T(128)} %bitcast.407, s32[]{:T(128)} %bitcast.408, s32[]{:T(128)} %bitcast.409, s32[]{:T(128)} %bitcast.410, s32[]{:T(128)} %bitcast.411, s32[]{:T(128)} %bitcast.412, s32[]{:T(128)} %bitcast.413, ...), kind=kLoop, calls=%fused_computation.49.clone.1 | loop fusion | flops 152576 | bytes 4356 | tf_op jit(solution)/shard_map/while/body/eval_jaxpr/jit(_take)/select_n | solution.py:42
  220.5 6.8 gather_fusion
  229.4 40.6 %select_select_fusion.4 = s32[1024]{0:T(1024)S(1)} fusion(s32[]{:T(128)} %bitcast.340, s32[]{:T(128)} %bitcast.341, s32[]{:T(128)} %bitcast.342, s32[]{:T(128)} %bitcast.343, s32[]{:T(128)} %bitcast.344, s32[]{:T(128)} %bitcast.345, s32[]{:T(128)} %bitcast.346, s32[]{:T(128)} %bitcast.347, s32[]{:T(128)} %bitcast.348, s32[]{:T(128)} %bitcast.349, ...), kind=kLoop, calls=%fused_computation.48.clone.1 | loop fusion | flops 152576 | bytes 4356 | tf_op jit(solution)/shard_map/while/body/eval_jaxpr/jit(_take)/select_n | solution.py:41
  276.7 40.3 %select_select_fusion.5 = s32[1024]{0:T(1024)S(1)} fusion(s32[]{:T(128)} %bitcast.404, s32[]{:T(128)} %bitcast.405, s32[]{:T(128)} %bitcast.406, s32[]{:T(128)} %bitcast.407, s32[]{:T(128)} %bitcast.408, s32[]{:T(128)} %bitcast.409, s32[]{:T(128)} %bitcast.410, s32[]{:T(128)} %bitcast.411, s32[]{:T(128)} %bitcast.412, s32[]{:T(128)} %bitcast.413, ...), kind=kLoop, calls=%fused_computation.49.clone.1 | loop fusion | flops 152576 | bytes 4356 | tf_op jit(solution)/shard_map/while/body/eval_jaxpr/jit(_take)/select_n | solution.py:42
  317.7 6.8 gather_fusion
  326.7 40.6 %select_select_fusion.4 = s32[1024]{0:T(1024)S(1)} fusion(s32[]{:T(128)} %bitcast.340, s32[]{:T(128)} %bitcast.341, s32[]{:T(128)} %bitcast.342, s32[]{:T(128)} %bitcast.343, s32[]{:T(128)} %bitcast.344, s32[]{:T(128)} %bitcast.345, s32[]{:T(128)} %bitcast.346, s32[]{:T(128)} %bitcast.347, s32[]{:T(128)} %bitcast.348, s32[]{:T(128)} %bitcast.349, ...), kind=kLoop, calls=%fused_computation.48.clone.1 | loop fusion | flops 152576 | bytes 4356 | tf_op jit(solution)/shard_map/while/body/eval_jaxpr/jit(_take)/select_n | solution.py:41
  374.0 40.3 %select_select_fusion.5 = s32[1024]{0:T(1024)S(1)} fusion(s32[]{:T(128)} %bitcast.404, s32[]{:T(128)} %bitcast.405, s32[]{:T(128)} %bitcast.406, s32[]{:T(128)} %bitcast.407, s32[]{:T(128)} %bitcast.408, s32[]{:T(128)} %bitcast.409, s32[]{:T(128)} %bitcast.410, s32[]{:T(128)} %bitcast.411, s32[]{:T(128)} %bitcast.412, s32[]{:T(128)} %bitcast.413, ...), kind=kLoop, calls=%fused_computation.49.clone.1 | loop fusion | flops 152576 | bytes 4356 | tf_op jit(solution)/shard_map/while/body/eval_jaxpr/jit(_take)/select_n | solution.py:42
  415.0 6.8 gather_fusion
  424.0 40.6 %select_select_fusion.4 = s32[1024]{0:T(1024)S(1)} fusion(s32[]{:T(128)} %bitcast.340, s32[]{:T(128)} %bitcast.341, s32[]{:T(128)} %bitcast.342, s32[]{:T(128)} %bitcast.343, s32[]{:T(128)} %bitcast.344, s32[]{:T(128)} %bitcast.345, s32[]{:T(128)} %bitcast.346, s32[]{:T(128)} %bitcast.347, s32[]{:T(128)} %bitcast.348, s32[]{:T(128)} %bitcast.349, ...), kind=kLoop, calls=%fused_computation.48.clone.1 | loop fusion | flops 152576 | bytes 4356 | tf_op jit(solution)/shard_map/while/body/eval_jaxpr/jit(_take)/select_n | solution.py:41
  471.2 40.3 %select_select_fusion.5 = s32[1024]{0:T(1024)S(1)} fusion(s32[]{:T(128)} %bitcast.404, s32[]{:T(128)} %bitcast.405, s32[]{:T(128)} %bitcast.406, s32[]{:T(128)} %bitcast.407, s32[]{:T(128)} %bitcast.408, s32[]{:T(128)} %bitcast.409, s32[]{:T(128)} %bitcast.410, s32[]{:T(128)} %bitcast.411, s32[]{:T(128)} %bitcast.412, s32[]{:T(128)} %bitcast.413, ...), kind=kLoop, calls=%fused_computation.49.clone.1 | loop fusion | flops 152576 | bytes 4356 | tf_op jit(solution)/shard_map/while/body/eval_jaxpr/jit(_take)/select_n | solution.py:42
  512.2 6.8 gather_fusion
  521.2 40.6 %select_select_fusion.4 = s32[1024]{0:T(1024)S(1)} fusion(s32[]{:T(128)} %bitcast.340, s32[]{:T(128)} %bitcast.341, s32[]{:T(128)} %bitcast.342, s32[]{:T(128)} %bitcast.343, s32[]{:T(128)} %bitcast.344, s32[]{:T(128)} %bitcast.345, s32[]{:T(128)} %bitcast.346, s32[]{:T(128)} %bitcast.347, s32[]{:T(128)} %bitcast.348, s32[]{:T(128)} %bitcast.349, ...), kind=kLoop, calls=%fused_computation.48.clone.1 | loop fusion | flops 152576 | bytes 4356 | tf_op jit(solution)/shard_map/while/body/eval_jaxpr/jit(_take)/select_n | solution.py:41
  568.5 40.3 %select_select_fusion.5 = s32[1024]{0:T(1024)S(1)} fusion(s32[]{:T(128)} %bitcast.404, s32[]{:T(128)} %bitcast.405, s32[]{:T(128)} %bitcast.406, s32[]{:T(128)} %bitcast.407, s32[]{:T(128)} %bitcast.408, s32[]{:T(128)} %bitcast.409, s32[]{:T(128)} %bitcast.410, s32[]{:T(128)} %bitcast.411, s32[]{:T(128)} %bitcast.412, s32[]{:T(128)} %bitcast.413, ...), kind=kLoop, calls=%fused_computation.49.clone.1 | loop fusion | flops 152576 | bytes 4356 | tf_op jit(solution)/shard_map/while/body/eval_jaxpr/jit(_take)/select_n | solution.py:42
  609.5 6.8 gather_fusion
  618.5 40.6 %select_select_fusion.4 = s32[1024]{0:T(1024)S(1)} fusion(s32[]{:T(128)} %bitcast.340, s32[]{:T(128)} %bitcast.341, s32[]{:T(128)} %bitcast.342, s32[]{:T(128)} %bitcast.343, s32[]{:T(128)} %bitcast.344, s32[]{:T(128)} %bitcast.345, s32[]{:T(128)} %bitcast.346, s32[]{:T(128)} %bitcast.347, s32[]{:T(128)} %bitcast.348, s32[]{:T(128)} %bitcast.349, ...), kind=kLoop, calls=%fused_computation.48.clone.1 | loop fusion | flops 152576 | bytes 4356 | tf_op jit(solution)/shard_map/while/body/eval_jaxpr/jit(_take)/select_n | solution.py:41
  665.8 40.3 %select_select_fusion.5 = s32[1024]{0:T(1024)S(1)} fusion(s32[]{:T(128)} %bitcast.404, s32[]{:T(128)} %bitcast.405, s32[]{:T(128)} %bitcast.406, s32[]{:T(128)} %bitcast.407, s32[]{:T(128)} %bitcast.408, s32[]{:T(128)} %bitcast.409, s32[]{:T(128)} %bitcast.410, s32[]{:T(128)} %bitcast.411, s32[]{:T(128)} %bitcast.412, s32[]{:T(128)} %bitcast.413, ...), kind=kLoop, calls=%fused_computation.49.clone.1 | loop fusion | flops 152576 | bytes 4356 | tf_op jit(solution)/shard_map/while/body/eval_jaxpr/jit(_take)/select_n | solution.py:42
  706.8 6.8 gather_fusion
  715.7 40.6 %select_select_fusion.4 = s32[1024]{0:T(1024)S(1)} fusion(s32[]{:T(128)} %bitcast.340, s32[]{:T(128)} %bitcast.341, s32[]{:T(128)} %bitcast.342, s32[]{:T(128)} %bitcast.343, s32[]{:T(128)} %bitcast.344, s32[]{:T(128)} %bitcast.345, s32[]{:T(128)} %bitcast.346, s32[]{:T(128)} %bitcast.347, s32[]{:T(128)} %bitcast.348, s32[]{:T(128)} %bitcast.349, ...), kind=kLoop, calls=%fused_computation.48.clone.1 | loop fusion | flops 152576 | bytes 4356 | tf_op jit(solution)/shard_map/while/body/eval_jaxpr/jit(_take)/select_n | solution.py:41
  757.7 1.5 fusion.87
  763.0 40.3 %select_select_fusion.5 = s32[1024]{0:T(1024)S(1)} fusion(s32[]{:T(128)} %bitcast.404, s32[]{:T(128)} %bitcast.405, s32[]{:T(128)} %bitcast.406, s32[]{:T(128)} %bitcast.407, s32[]{:T(128)} %bitcast.408, s32[]{:T(128)} %bitcast.409, s32[]{:T(128)} %bitcast.410, s32[]{:T(128)} %bitcast.411, s32[]{:T(128)} %bitcast.412, s32[]{:T(128)} %bitcast.413, ...), kind=kLoop, calls=%fused_computation.49.clone.1 | loop fusion | flops 152576 | bytes 4356 | tf_op jit(solution)/shard_map/while/body/eval_jaxpr/jit(_take)/select_n | solution.py:42
  804.0 6.8 gather_fusion
  813.0 40.6 %select_select_fusion.4 = s32[1024]{0:T(1024)S(1)} fusion(s32[]{:T(128)} %bitcast.340, s32[]{:T(128)} %bitcast.341, s32[]{:T(128)} %bitcast.342, s32[]{:T(128)} %bitcast.343, s32[]{:T(128)} %bitcast.344, s32[]{:T(128)} %bitcast.345, s32[]{:T(128)} %bitcast.346, s32[]{:T(128)} %bitcast.347, s32[]{:T(128)} %bitcast.348, s32[]{:T(128)} %bitcast.349, ...), kind=kLoop, calls=%fused_computation.48.clone.1 | loop fusion | flops 152576 | bytes 4356 | tf_op jit(solution)/shard_map/while/body/eval_jaxpr/jit(_take)/select_n | solution.py:41
  857.7 81.0 %all-reduce.2.cloned.1.call-done = bf16[128,256]{1,0:T(8,128)(2,1)} async-done(((bf16[128,256]{1,0:T(8,128)(2,1)}), bf16[128,256]{1,0:T(8,128)(2,1)}) %all-reduce.2.cloned.1.call-update) | async-done | bytes 65552 | tf_op jit(solution)/shard_map/psum | solution.py:91
  938.7 1.5 copy.26
  (202 shorter events, 77.0 us)
Async XLA Ops:
  6.5 850.2 %copy-start = (bf16[128,256]{1,0:T(8,128)(2,1)S(1)}, bf16[128,256]{1,0:T(8,128)(2,1)}, u32[]{:S(2)}) copy-start(bf16[128,256]{1,0:T(8,128)(2,1)} %param.15) | copy-start | bytes 196612
  9.2 67.5 %all-to-all-start = ((bf16[64,128,128]{2,1,0:T(8,128)(2,1)}), bf16[64,128,128]{2,1,0:T(8,128)(2,1)S(1)}, u32[]{:S(2)}, u32[]{:S(2)}) async-start(bf16[64,128,128]{2,1,0:T(8,128)(2,1)} %stack.2), calls=%async_computation | async-start | bytes 4194304 | tf_op jit(solution)/shard_map/all_to_all | solution.py:74
  28.3 1.7 copy-start.3
  28.3 1.7 copy-start.4
  28.3 1.8 copy-start.1
  28.3 2.1 copy-start.5
  28.3 910.3 %all-reduce.2.cloned.1.call-start = ((), (), s32[]{:S(2)}) async-start(), calls=%async_computation.1 | async-start | bytes 131072 | tf_op jit(solution)/shard_map/psum | solution.py:91
  76.7 0.7 copy-start.6
  77.4 1.3 copy-start.2
Sparse Core Ops, SparseCore 0:
  857.8 80.8 all-reduce.1
